TPU v7x, 32 devices: a whole 2x2x4 slice. The times are simulated.
32 devices in a mesh: rows: 4 (over y, core), chan: 8 (over z, x).
Axes of the slice: x: 2, y: 2, z: 4, core: 2. Of those that a mesh axis runs over, the one named last changes fastest.
Arguments:
- features: bfloat16 [1024, 16, 128], P('chan', 'rows'), may hold values from -6 to 6
- hidden: bfloat16 [1024, 16, 128], P('chan', 'rows'), may hold values from -1 to 1
- w_update: bfloat16 [3, 3, 1024, 2048], P(None, None, 'chan'), may hold values from -0.046875 to 0.046875
- w_reset: bfloat16 [3, 3, 1024, 2048], P(None, None, 'chan'), may hold values from -0.046875 to 0.046875
- w_cand: bfloat16 [3, 3, 1024, 2048], P(None, None, 'chan'), may hold values from -0.046875 to 0.046875
- b_update: float32 [1024], P('chan'), may hold values from -1 to 1
- b_reset: float32 [1024], P('chan'), may hold values from -1 to 1
- b_cand: float32 [1024], P('chan'), may hold values from -1 to 1
Outputs:
- new_hidden: bfloat16 [1024, 16, 128], P('chan', 'rows')
All inputs are finite; a program needn't handle non-finite values.
Results may differ from a plain program's by a relative error of at most 0.0018.
Values may be sent and summed in bfloat16 or wider, within the bound.
A program may use at most 128 MiB of HBM per device.

v0:
```python
import functools

import jax
import jax.numpy as jnp
from jax import lax
from jax.experimental import pallas as pl
from jax.experimental.pallas import tpu as pltpu
from jax.sharding import PartitionSpec as P

MESH = pl.DeviceIdType.MESH
PAIR = 2


def kernel(
    n_chan, n_rows, cols,
    features, hidden, b_update, b_reset, b_cand, w_update, w_reset, w_cand,
    out,
    joined, rh, rh_loc, weights, acc, acc_cand, gate,
    w_sem, own_sem, send1, band1, rim1, send2, band2, rim2,
):
    n = features.shape[0]
    band = features.shape[1]
    channels = joined.shape[1]
    lines = n_chan // PAIR
    me = lax.axis_index("chan")
    row = lax.axis_index("rows")
    line, pair = me // PAIR, me % PAIR
    has_up, has_down = line < lines - 1, line > 0
    has_above, has_below = row > 0, row < n_rows - 1

    w_copies = [
        pltpu.make_async_copy(src, weights.at[i], w_sem.at[i])
        for i, src in enumerate((w_reset, w_update, w_cand))
    ]
    for copy in w_copies:
        copy.start()

    def ident(l, p):
        return l * PAIR + p

    up, down, partner = ident(line + 1, pair), ident(line - 1, pair), ident(line, 1 - pair)
    barrier = pltpu.get_barrier_semaphore()

    def greet(there, target):
        @pl.when(there)
        def _():
            pl.semaphore_signal(barrier, inc=1, device_id=target, device_id_type=MESH)

    pl.semaphore_signal(barrier, inc=1, device_id={"chan": partner}, device_id_type=MESH)
    greet(has_up, {"chan": up})
    greet(has_down, {"chan": down})
    greet(has_above, {"rows": row - 1})
    greet(has_below, {"rows": row + 1})
    pl.semaphore_wait(
        barrier,
        1
        + has_up.astype(jnp.int32)
        + has_down.astype(jnp.int32)
        + has_above.astype(jnp.int32)
        + has_below.astype(jnp.int32),
    )

    def mover(own, dest, own_sem, send, band_sem, rim_sem):
        def band_copy(kind, c, h, mine, target):
            dst = dest(c, h, cols, band)
            return pltpu.make_async_remote_copy(
                src_ref=own(h, 0, band) if mine else dst,
                dst_ref=dst,
                send_sem=send.at[kind, c, h],
                recv_sem=band_sem.at[c, h],
                device_id={"chan": target},
                device_id_type=MESH,
            )

        def rim_copy(side, c, h, mine):
            first = 0 if side == 0 else band - cols
            return pltpu.make_async_remote_copy(
                src_ref=own(h, first, cols) if mine else dest(c, h, cols + first, cols),
                dst_ref=dest(c, h, cols + band if side == 0 else 0, cols),
                send_sem=send.at[3 + side, c, h],
                recv_sem=rim_sem.at[side, c, h],
                device_id={"rows": row - 1 if side == 0 else row + 1},
                device_id_type=MESH,
            )

        def start(copy):
            copy.start()

        def done(copy):
            copy.wait_send()

        def rims(c, h, mine, act):
            @pl.when(has_above)
            def _():
                act(rim_copy(0, c, h, mine))

            @pl.when(has_below)
            def _():
                act(rim_copy(1, c, h, mine))

        def send_line(kind, ok, c, h, mine, act):
            @pl.when(ok)
            def _():
                act(band_copy(kind, c, h, mine, up if kind == 0 else down))

        def local(h):
            return pltpu.make_async_copy(own(h, 0, band), dest(me, h, cols, band), own_sem.at[h])

        def begin(act):
            for h in range(2):
                send_line(0, has_up, me, h, True, act)
                send_line(1, has_down, me, h, True, act)
                act(band_copy(2, me, h, True, partner))
            for h in range(2):
                rims(me, h, True, act)

        def from_below(s, h, act, first):
            c = ident(line - s, pair)

            @pl.when(line >= s)
            def _():
                if first:
                    band_copy(0, c, h, False, partner).wait_recv()
                send_line(0, has_up, c, h, False, act)
                act(band_copy(2, c, h, False, partner))
                rims(c, h, False, act)

        def from_above(s, h, act, first):
            c = ident(line + s, pair)

            @pl.when(line + s < lines)
            def _():
                if first:
                    band_copy(0, c, h, False, partner).wait_recv()
                send_line(1, has_down, c, h, False, act)
                act(band_copy(2, c, h, False, partner))
                rims(c, h, False, act)

        def from_pair(l, ok, act, first):
            c = ident(l, 1 - pair)

            @pl.when(ok)
            def _():
                for h in range(2):
                    if first:
                        band_copy(2, c, h, False, partner).wait_recv()
                    rims(c, h, False, act)

        def ready(c):
            for h in range(2):
                @pl.when(has_below)
                def _():
                    rim_copy(0, c, h, False).wait_recv()

                @pl.when(has_above)
                def _():
                    rim_copy(1, c, h, False).wait_recv()

        def across(s, act, first):
            from_pair(line - s, line >= s, act, first)
            if s > 0:
                from_pair(line + s, line + s < lines, act, first)

        def run(compute):
            eager = n % 128 == 0

            def use(s, p):
                if not eager:
                    return
                for l, ok in (
                    (line - s, line >= s),
                    (line + s, line + s < lines),
                )[: 1 if s == 0 else 2]:
                    @pl.when(ok)
                    def _():
                        c = ident(l, p)
                        ready(c)
                        compute(c)

            for h in range(2):
                local(h).wait()
            for s in range(1, lines):
                for h in range(2):
                    from_below(s, h, start, True)
                    from_above(s, h, start, True)
                across(s - 1, start, True)
                use(s - 1, pair)
                if s >= 2:
                    use(s - 2, 1 - pair)
            if lines >= 2:
                use(lines - 2, 1 - pair)
            use(lines - 1, pair)
            across(lines - 1, start, True)
            use(lines - 1, 1 - pair)
            if not eager:
                for c in range(n_chan):
                    ready(c)
                for g in range(channels // 128):
                    compute(g)

        def finish():
            begin(done)
            for s in range(1, lines):
                for h in range(2):
                    from_below(s, h, done, False)
                    from_above(s, h, done, False)
            for s in range(lines):
                across(s, done, False)

        def launch():
            begin(start)
            for h in range(2):
                local(h).start()

        return launch, run, finish

    def own1(h, start, size):
        return (features, hidden)[h].at[:, pl.ds(start, size)]

    def dest1(c, h, start, size):
        return joined.at[h, pl.ds(pl.multiple_of(c * n, n), n), pl.ds(start, size)]

    half = n // 2

    def own2(h, start, size):
        return rh_loc.at[pl.ds(h * half, half), pl.ds(start, size)]

    def dest2(c, h, start, size):
        return rh.at[
            0, pl.ds(pl.multiple_of(c * n + h * half, half), half), pl.ds(start, size)
        ]

    launch1, run1, finish1 = mover(own1, dest1, own_sem.at[0], send1, band1, rim1)
    launch2, run2, finish2 = mover(own2, dest2, own_sem.at[1], send2, band2, rim2)
    launch1()

    @pl.when(jnp.logical_not(has_above))
    def _():
        for buf in (joined, rh):
            buf[:, :, pl.ds(0, cols)] = jnp.zeros((buf.shape[0], channels, cols), buf.dtype)

    @pl.when(jnp.logical_not(has_below))
    def _():
        for buf in (joined, rh):
            buf[:, :, pl.ds(cols + band, cols)] = jnp.zeros(
                (buf.shape[0], channels, cols), buf.dtype
            )

    def part(gates, parts, ks_list, buf, bufs, g):
        ks = pl.ds(pl.multiple_of(g * 128, 128), 128)
        left, right = [], []
        for a in range(3):
            for offset, b in zip(ks_list, bufs):
                kw = pl.ds(pl.multiple_of(offset + g * 128, 128), 128)
                w = weights[pl.ds(gates, parts), a, :, :, kw]
                left.append(w.reshape(parts * 3 * n, 128))
                right.append(buf[b, ks, pl.ds(a * cols, band)])
        return jnp.dot(
            jnp.concatenate(left, 1),
            jnp.concatenate(right, 0),
            preferred_element_type=jnp.float32,
        )

    acc[...] = jnp.zeros_like(acc)
    for copy in w_copies:
        copy.wait()

    def gates_on(g):
        for i in range(2):
            acc[i] += part(i, 1, (0, channels), joined, (0, 1), g)

    run1(gates_on)

    lane = lax.broadcasted_iota(jnp.int32, (n, cols), 1)

    diagonal = lax.broadcasted_iota(jnp.int32, (n, n), 0) == lax.broadcasted_iota(
        jnp.int32, (n, n), 1
    )

    def column(ref):
        return jnp.sum(jnp.where(diagonal, ref[...], 0.0), axis=1, keepdims=True)

    def folded(ref, i, r):
        cells = pl.ds(r * cols, cols)
        low = pltpu.roll(ref[i, pl.ds(0, n), cells], 1, 1)
        mid = ref[i, pl.ds(n, n), cells]
        high = pltpu.roll(ref[i, pl.ds(2 * n, n), cells], cols - 1, 1)
        return jnp.where(lane == 0, 0.0, low) + mid + jnp.where(lane == cols - 1, 0.0, high)

    for r in range(band // cols):
        cells = pl.ds(r * cols, cols)
        reset = jax.nn.sigmoid(folded(acc, 0, r) + column(b_reset))
        rh_loc[:, cells] = (reset * hidden[:, cells].astype(jnp.float32)).astype(rh_loc.dtype)
    launch2()

    for r in range(band // cols):
        gate[:, pl.ds(r * cols, cols)] = jax.nn.sigmoid(folded(acc, 1, r) + column(b_update))
    acc_cand[0] = part(2, 1, (0,), joined, (0,), 0)

    @pl.loop(1, channels // 128)
    def _(g):
        acc_cand[0] += part(2, 1, (0,), joined, (0,), g)

    def cand_on(g):
        acc_cand[0] += part(2, 1, (channels,), rh, (0,), g)

    run2(cand_on)

    for r in range(band // cols):
        cells = pl.ds(r * cols, cols)
        candidate = jnp.tanh(folded(acc_cand, 0, r) + column(b_cand))
        update = gate[:, cells]
        out[:, cells] = (
            (1.0 - update) * hidden[:, cells].astype(jnp.float32) + update * candidate
        ).astype(out.dtype)
    finish1()
    finish2()


def per_device(n_chan, n_rows, features, hidden, w_update, w_reset, w_cand, b_update, b_reset, b_cand):
    n, rows, cols = features.shape
    band = rows * cols
    channels = n * n_chan
    wide = band + 2 * cols
    bf16, f32 = jnp.bfloat16, jnp.float32
    vmem = pl.BlockSpec(memory_space=pltpu.VMEM)
    hbm = pl.BlockSpec(memory_space=pl.ANY)
    dma = pltpu.SemaphoreType.DMA
    result = pl.pallas_call(
        functools.partial(kernel, n_chan, n_rows, cols),
        out_shape=jax.ShapeDtypeStruct((n, band), bf16),
        in_specs=[vmem] * 5 + [hbm] * 3,
        out_specs=vmem,
        scratch_shapes=[
            pltpu.VMEM((2, channels, wide), bf16),
            pltpu.VMEM((1, channels, wide), bf16),
            pltpu.VMEM((n, band), bf16),
            pltpu.VMEM((3,) + w_update.shape, bf16),
            pltpu.VMEM((2, 3 * n, band), f32),
            pltpu.VMEM((1, 3 * n, band), f32),
            pltpu.VMEM((n, band), f32),
            dma((3,)),
            dma((2, 2)),
            dma((5, n_chan, 2)),
            dma((n_chan, 2)),
            dma((2, n_chan, 2)),
            dma((5, n_chan, 2)),
            dma((n_chan, 2)),
            dma((2, n_chan, 2)),
        ],
        compiler_params=pltpu.CompilerParams(
            collective_id=0, has_side_effects=True, vmem_limit_bytes=60 * 1024 * 1024
        ),
    )(
        features.reshape(n, band),
        hidden.reshape(n, band),
        b_update.reshape(1, n),
        b_reset.reshape(1, n),
        b_cand.reshape(1, n),
        w_update,
        w_reset,
        w_cand,
    )
    return result.reshape(n, rows, cols)


def solution(mesh):
    in_specs = (
        P("chan", "rows", None),
        P("chan", "rows", None),
        P(None, None, "chan", None),
        P(None, None, "chan", None),
        P(None, None, "chan", None),
        P("chan"),
        P("chan"),
        P("chan"),
    )
    return jax.shard_map(
        functools.partial(per_device, mesh.shape["chan"], mesh.shape["rows"]),
        mesh=mesh,
        in_specs=in_specs,
        out_specs=P("chan", "rows", None),
        check_vma=False,
    )
```

profile of v0, /device:TPU:1, one launch (start us, length us, event | category | flops | bytes accessed | tf_op | source)
XLA Modules:
  0.0 57.0 jit_solution(16717736282393652343)
XLA Ops:
  0.0 1.7 %copy_bitcast_fusion = (bf16[128,512]{1,0:T(8,128)(2,1)}, bf16[128,512]{1,0:T(8,128)(2,1)}) fusion(bf16[16,8,4,128]{3,2,1,0:T(4,128)(2,1)} %bitcast.9, bf16[16,8,4,128]{3,2,1,0:T(4,128)(2,1)} %bitcast.10), kind=kLoop, calls=%fused_computation | loop fusion | bytes 524288 | tf_op jit(solution)/shard_map/reshape | solution.py:356
  1.7 53.7 %shard_map.82 = bf16[128,512]{1,0:T(8,128)(2,1)} custom-call(bf16[128,512]{1,0:T(8,128)(2,1)} %get-tuple-element.6.features, bf16[128,512]{1,0:T(8,128)(2,1)} %get-tuple-element.5.hidden, f32[1,128]{1,0:T(1,128)} %bitcast.11, f32[1,128]{1,0:T(1,128)} %bitcast.12, f32[1,128]{1,0:T(1,128)} %bitcast.13, bf16[3,3,128,2048]{3,2,1,0:T(8,128)(2,1)} %w_update.1, ...), custom_call_target="tpu_custom_call" | custom-call | tf_op jit(solution)/shard_map/pallas_call | solution.py:329
  55.4 1.6 %reshape.23 = bf16[128,4,128]{2,1,0:T(4,128)(2,1)} reshape(bf16[128,512]{1,0:T(8,128)(2,1)} %shard_map.82) | data formatting | bytes 262144 | tf_op jit(solution)/shard_map/reshape | solution.py:364
where the time goes:
time: 57.2 us; the launch traced here: 57 us
  Pallas kernels  53.7 us (94%)
  local copies, waits for them, and re-layouts  3.28 us (6%)
    pallas_call x1, Pallas kernels, per_device(): pl.pallas_call(functools.partial(kernel, n_chan, n_rows, cols), out_shape...  53.7 us
    reshape x1, local copies, waits for them, and re-layouts, per_device(): hidden.reshape(n, band)  1.69 us
    reshape x1, local copies, waits for them, and re-layouts, per_device(): return result.reshape(n, rows, cols)  1.59 us

commit v1 on v0

v1 whole, which is shorter than its diff:
```python
import functools

import jax
import jax.numpy as jnp
from jax import lax
from jax.experimental import pallas as pl
from jax.experimental.pallas import tpu as pltpu
from jax.sharding import PartitionSpec as P

MESH = pl.DeviceIdType.MESH
PAIR = 2
WIDE = 128
EDGE, INNER = 0, 1


def kernel(
    n_chan, n_rows, rows,
    features, hidden, b_update, b_reset, b_cand, w_update, w_reset, w_cand,
    out,
    raw, joined, rh, weights, acc, acc_cand, gate, bias,
    raw_sem, w_sem, send1, band1, rim1, send2, band2, rim2,
):
    cols = raw.shape[-1]
    channels = joined.shape[2]
    n = channels // n_chan
    lines = n_chan // PAIR
    me = lax.axis_index("chan")
    row = lax.axis_index("rows")
    line, pair = me // PAIR, me % PAIR
    has_up, has_down = line < lines - 1, line > 0
    has_above, has_below = row > 0, row < n_rows - 1
    eager = n % WIDE == 0
    f32 = jnp.float32

    raw_copies = [
        pltpu.make_async_copy(src, raw.at[i], raw_sem.at[i])
        for i, src in enumerate((features, hidden))
    ]
    w_copies = [
        pltpu.make_async_copy(src, weights.at[i], w_sem.at[i])
        for i, src in enumerate((w_reset, w_update, w_cand))
    ]
    for copy in raw_copies + w_copies:
        copy.start()

    def ident(l, p):
        return l * PAIR + p

    up, down, partner = ident(line + 1, pair), ident(line - 1, pair), ident(line, 1 - pair)
    barrier = pltpu.get_barrier_semaphore()

    def greet(there, target):
        @pl.when(there)
        def _():
            pl.semaphore_signal(barrier, inc=1, device_id=target, device_id_type=MESH)

    pl.semaphore_signal(barrier, inc=1, device_id={"chan": partner}, device_id_type=MESH)
    greet(has_up, {"chan": up})
    greet(has_down, {"chan": down})
    greet(has_above, {"rows": row - 1})
    greet(has_below, {"rows": row + 1})

    def slot(r):
        if r == -1 or r == rows:
            return rows + (r == rows)
        return {0: 0, rows - 1: 1}.get(r, r + 1)

    def block(c):
        return pl.ds(pl.multiple_of(c * n, n), n)

    mine = block(me)

    def iota(shape, axis):
        return lax.broadcasted_iota(jnp.int32, shape, axis)

    to_planes = jnp.concatenate(
        [
            (iota((n, n * rows), 0) * rows + r == iota((n, n * rows), 1)).astype(f32)
            for r in range(rows)
        ],
        0,
    ).astype(raw.dtype)
    for i, copy in enumerate(raw_copies):
        copy.wait()
        planes = jnp.dot(to_planes, raw[i], preferred_element_type=f32).astype(raw.dtype)
        for r in range(rows):
            joined[i, slot(r), mine] = planes[r * n : (r + 1) * n]

    pl.semaphore_wait(
        barrier,
        1
        + has_up.astype(jnp.int32)
        + has_down.astype(jnp.int32)
        + has_above.astype(jnp.int32)
        + has_below.astype(jnp.int32),
    )

    class Mover:
        def __init__(self, buf, send, band_sem, rim_sem):
            self.buf, self.send, self.band_sem, self.rim_sem = buf, send, band_sem, rim_sem
            self.kinds = range(buf.shape[0])

        def band(self, way, c, part, h):
            slots = pl.ds(0, 2) if part == EDGE else pl.ds(2, rows - 2)
            ref = self.buf.at[h, slots, block(c)]
            return pltpu.make_async_remote_copy(
                src_ref=ref,
                dst_ref=ref,
                send_sem=self.send.at[way, c, part, h],
                recv_sem=self.band_sem.at[c, part, h],
                device_id={"chan": (up, down, partner)[way]},
                device_id_type=MESH,
            )

        def rim(self, side, c, h):
            return pltpu.make_async_remote_copy(
                src_ref=self.buf.at[h, side, block(c)],
                dst_ref=self.buf.at[h, rows + 1 - side, block(c)],
                send_sem=self.send.at[3 + side, c, EDGE, h],
                recv_sem=self.rim_sem.at[side, c, h],
                device_id={"rows": row - 1 if side == 0 else row + 1},
                device_id_type=MESH,
            )

        def rims(self, c, h, act):
            @pl.when(has_above)
            def _():
                act(self.rim(0, c, h))

            @pl.when(has_below)
            def _():
                act(self.rim(1, c, h))

        def along(self, way, c, part, h, act):
            @pl.when((has_up, has_down)[way])
            def _():
                act(self.band(way, c, part, h))

        def begin(self, act, part):
            for h in self.kinds:
                self.along(0, me, part, h, act)
                self.along(1, me, part, h, act)
                act(self.band(2, me, part, h))
            if part == EDGE:
                for h in self.kinds:
                    self.rims(me, h, act)

        def pass_on(self, s, act, first):
            for part in (EDGE, INNER):
                for h in self.kinds:
                    for way, l in ((0, line - s), (1, line + s)):
                        @pl.when((l >= 0) & (l < lines))
                        def _():
                            c = ident(l, pair)
                            if first:
                                self.band(2, c, part, h).wait_recv()
                            self.along(way, c, part, h, act)
                            if part == EDGE or s > 1:
                                act(self.band(2, c, part, h))
                            if part == EDGE:
                                self.rims(c, h, act)

        def diagonal(self, act):
            for h in self.kinds:
                self.along(0, partner, INNER, h, act)
                self.along(1, partner, INNER, h, act)

        def across(self, s, act, first):
            for l in (line - s, line + s)[: 1 if s == 0 else 2]:
                @pl.when((l >= 0) & (l < lines))
                def _():
                    c = ident(l, 1 - pair)
                    for h in self.kinds:
                        if first:
                            self.band(2, c, EDGE, h).wait_recv()
                        self.rims(c, h, act)

        def rims_in(self, c):
            for h in self.kinds:
                @pl.when(has_below)
                def _():
                    self.rim(0, c, h).wait_recv()

                @pl.when(has_above)
                def _():
                    self.rim(1, c, h).wait_recv()

        def inner_in(self, c):
            for h in self.kinds:
                self.band(2, c, INNER, h).wait_recv()

        def finish(self):
            for part in (EDGE, INNER):
                self.begin(done, part)
            for s in range(1, lines):
                self.pass_on(s, done, False)
            self.diagonal(done)
            for s in range(lines):
                self.across(s, done, False)

    def start(copy):
        copy.start()

    def done(copy):
        copy.wait_send()

    def sides(s, body):
        @pl.loop(0, 2)
        def _(j):
            l = line + (2 * j - 1) * s

            @pl.when((l >= 0) & (l < lines))
            def _():
                body(l)

    first, second = Mover(joined, send1, band1, rim1), Mover(rh, send2, band2, rim2)
    for part in (EDGE, INNER):
        first.begin(start, part)

    for there, r in ((has_above, -1), (has_below, rows)):
        @pl.when(jnp.logical_not(there))
        def _():
            for buf in (joined, rh):
                for h in range(buf.shape[0]):
                    buf[h, slot(r)] = jnp.zeros((channels, cols), buf.dtype)

    diagonal = iota((n, n), 0) == iota((n, n), 1)
    for i, ref in enumerate((b_reset, b_update, b_cand)):
        column = jnp.sum(jnp.where(diagonal, ref[...], 0.0), axis=1, keepdims=True)
        bias[i] = jnp.broadcast_to(column, (n, cols))
    acc_cand[...] = jnp.zeros_like(acc_cand)
    if not eager:
        acc[...] = jnp.zeros_like(acc)

    def product(gates, count, sources, at, width):
        left, right = [], []
        for a in range(3):
            for offset, buf, h in sources:
                kw = pl.ds(pl.multiple_of(offset + at, WIDE), width)
                ks = pl.ds(pl.multiple_of(at, WIDE), width)
                left.append(
                    weights[pl.ds(gates, count), a, :, :, kw].reshape(count * 3 * n, width)
                )
                right.append(
                    jnp.concatenate([buf[h, slot(r + a - 1), ks] for r in range(rows)], 1)
                )
        return jnp.dot(
            jnp.concatenate(left, 1),
            jnp.concatenate(right, 0),
            preferred_element_type=f32,
        )

    both = ((0, joined, 0), (channels, joined, 1))
    size = 3 * n

    def gates_on(c):
        acc[...] += product(0, 2, both, c * n, n)

    def reset_on(c):
        acc[pl.ds(0, size)] += product(0, 1, both, c * n, n)

    def update_on(c):
        acc[pl.ds(size, size)] += product(1, 1, both, c * n, n)

    def old_on(at, width):
        acc_cand[...] += product(2, 1, ((0, joined, 0),), at, width)

    def new_on(at, width):
        acc_cand[...] += product(2, 1, ((channels, rh, 0),), at, width)

    last = sorted({1, lines - 1})

    def near(s):
        def body(l):
            c = ident(l, pair)
            first.rims_in(c)
            gates_on(c)

        sides(s, body)

    def far(s, compute):
        def body(l):
            c = ident(l, 1 - pair)
            first.inner_in(c)
            first.rims_in(c)
            compute(c)

        sides(s, body)

    for s in range(1, lines):
        first.pass_on(s, start, True)
        if s == max(1, lines - 2):
            if s == 1:
                first.inner_in(partner)
            first.diagonal(start)
        first.across(s - 1, start, True)
        if s == 1:
            if lines > 3:
                first.inner_in(partner)
            w_copies[0].wait()
            w_copies[1].wait()
            if eager:
                first.rims_in(me)
                acc[...] = product(0, 2, both, me * n, n)
                first.rims_in(partner)
                gates_on(partner)
        elif eager:
            near(s - 1)
            if s > 2:
                far(s - 1, gates_on)
    first.across(lines - 1, start, True)
    if eager:
        near(lines - 1)
        for s in last:
            far(s, reset_on)
    else:
        for s in range(1, lines):
            sides(s, lambda l: first.inner_in(ident(l, 1 - pair)))

        @pl.loop(0, n_chan)
        def _(c):
            first.rims_in(c)

        @pl.loop(0, channels // WIDE)
        def _(g):
            acc[...] += product(0, 2, both, g * WIDE, WIDE)

    lane = iota((n, cols), 1)

    def folded(ref, i, r):
        cells = pl.ds(r * cols, cols)
        low = pltpu.roll(ref[pl.ds(i * size, n), cells], 1, 1)
        mid = ref[pl.ds(i * size + n, n), cells]
        high = pltpu.roll(ref[pl.ds(i * size + 2 * n, n), cells], cols - 1, 1)
        return jnp.where(lane == 0, 0.0, low) + mid + jnp.where(lane == cols - 1, 0.0, high)

    def own_hidden(r):
        return joined[1, slot(r), mine].astype(f32)

    for part, inside in ((EDGE, (0, rows - 1)), (INNER, range(1, rows - 1))):
        for r in inside:
            reset = jax.nn.sigmoid(folded(acc, 0, r) + bias[0])
            rh[0, slot(r), mine] = (reset * own_hidden(r)).astype(rh.dtype)
        second.begin(start, part)

    if eager:
        for s in last:
            sides(s, lambda l: update_on(ident(l, 1 - pair)))
    w_copies[2].wait()

    def older():
        width = PAIR * n if eager else WIDE

        @pl.loop(0, channels // width)
        def _(g):
            old_on(g * width, width)

        for r in range(rows):
            gate[r] = jax.nn.sigmoid(folded(acc, 1, r) + bias[1])

    def both_on(l):
        for p in range(PAIR):
            second.rims_in(ident(l, p))
        new_on(l * PAIR * n, PAIR * n)

    def both_far(s):
        def body(l):
            second.inner_in(ident(l, 1 - pair))
            both_on(l)

        sides(s, body)

    for s in range(1, lines):
        second.pass_on(s, start, True)
        if s == max(1, lines - 2):
            if s == 1:
                second.inner_in(partner)
            second.diagonal(start)
        second.across(s - 1, start, True)
        if s == 1:
            if lines > 3:
                second.inner_in(partner)
            older()
            if eager:
                both_on(line)
        elif eager and s > 2:
            both_far(s - 1)
    second.across(lines - 1, start, True)
    if eager:
        for s in last:
            both_far(s)
    else:
        for s in range(1, lines):
            sides(s, lambda l: second.inner_in(ident(l, 1 - pair)))

        @pl.loop(0, n_chan)
        def _(c):
            second.rims_in(c)

        @pl.loop(0, channels // WIDE)
        def _(g):
            new_on(g * WIDE, WIDE)

    fresh = []
    for r in range(rows):
        candidate = jnp.tanh(folded(acc_cand, 0, r) + bias[2])
        update = gate[r]
        fresh.append(((1.0 - update) * own_hidden(r) + update * candidate).astype(out.dtype))
    from_planes = jnp.concatenate(
        [
            (iota((n * rows, n), 0) == iota((n * rows, n), 1) * rows + r).astype(f32)
            for r in range(rows)
        ],
        1,
    ).astype(out.dtype)
    out[...] = jnp.dot(
        from_planes, jnp.concatenate(fresh, 0), preferred_element_type=f32
    ).astype(out.dtype)
    first.finish()
    second.finish()


def per_device(n_chan, n_rows, features, hidden, w_update, w_reset, w_cand, b_update, b_reset, b_cand):
    n, rows, cols = features.shape
    band = rows * cols
    channels = n * n_chan
    bf16, f32 = jnp.bfloat16, jnp.float32
    vmem = pl.BlockSpec(memory_space=pltpu.VMEM)
    hbm = pl.BlockSpec(memory_space=pl.ANY)
    dma = pltpu.SemaphoreType.DMA
    result = pl.pallas_call(
        functools.partial(kernel, n_chan, n_rows, rows),
        out_shape=jax.ShapeDtypeStruct((n * rows, cols), bf16),
        in_specs=[hbm] * 2 + [vmem] * 3 + [hbm] * 3,
        out_specs=vmem,
        scratch_shapes=[
            pltpu.VMEM((2, n * rows, cols), bf16),
            pltpu.VMEM((2, rows + 2, channels, cols), bf16),
            pltpu.VMEM((1, rows + 2, channels, cols), bf16),
            pltpu.VMEM((3,) + w_update.shape, bf16),
            pltpu.VMEM((6 * n, band), f32),
            pltpu.VMEM((3 * n, band), f32),
            pltpu.VMEM((rows, n, cols), f32),
            pltpu.VMEM((3, n, cols), f32),
            dma((2,)),
            dma((3,)),
            dma((5, n_chan, 2, 2)),
            dma((n_chan, 2, 2)),
            dma((2, n_chan, 2)),
            dma((5, n_chan, 2, 1)),
            dma((n_chan, 2, 1)),
            dma((2, n_chan, 1)),
        ],
        compiler_params=pltpu.CompilerParams(
            collective_id=0, has_side_effects=True, vmem_limit_bytes=60 * 1024 * 1024
        ),
    )(
        features.reshape(n * rows, cols),
        hidden.reshape(n * rows, cols),
        b_update.reshape(1, n),
        b_reset.reshape(1, n),
        b_cand.reshape(1, n),
        w_update,
        w_reset,
        w_cand,
    )
    return result.reshape(n, rows, cols)


def solution(mesh):
    in_specs = (
        P("chan", "rows", None),
        P("chan", "rows", None),
        P(None, None, "chan", None),
        P(None, None, "chan", None),
        P(None, None, "chan", None),
        P("chan"),
        P("chan"),
        P("chan"),
    )
    return jax.shard_map(
        functools.partial(per_device, mesh.shape["chan"], mesh.shape["rows"]),
        mesh=mesh,
        in_specs=in_specs,
        out_specs=P("chan", "rows", None),
        check_vma=False,
    )
```

time: 57.2 us -> 57.2 us (level)
  Pallas kernels: 53.7 us -> 55.4 us
  local copies, waits for them, and re-layouts: 3.28 us -> 1.61 us
    reshape x2 -> x0, local copies, waits for them, and re-layouts: 3.28 us -> none  [the longest x1 1.69 us: per_device(): hidden.reshape(n, band)]
    pallas_call x1, Pallas kernels: 53.7 us -> 55.4 us  [per_device(): pl.pallas_call(functools.partial(kernel, n_chan, n_rows, rows), out_shape...]
    unnamed x0 -> x1, local copies, waits for them, and re-layouts: none -> 1.61 us
where the time goes in v1:
time: 57.2 us; the launch traced here: 57 us
  Pallas kernels  55.4 us (97%)
  local copies, waits for them, and re-layouts  1.61 us (3%)
    pallas_call x1, Pallas kernels, per_device(): pl.pallas_call(functools.partial(kernel, n_chan, n_rows, rows), out_shape...  55.4 us
    unnamed x1, local copies, waits for them, and re-layouts  1.61 us

profile of v1, /device:TPU:1, one launch (start us, length us, event | category | flops | bytes accessed | tf_op | source)
XLA Modules:
  0.0 57.0 jit_solution(7908284648909512853)
XLA Ops:
  0.0 55.4 %shard_map.82 = bf16[512,128]{1,0:T(8,128)(2,1)} custom-call(bf16[512,128]{1,0:T(8,128)(2,1)} %bitcast.7, bf16[512,128]{1,0:T(8,128)(2,1)} %bitcast.8, f32[1,128]{1,0:T(1,128)} %bitcast.9, f32[1,128]{1,0:T(1,128)} %bitcast.10, f32[1,128]{1,0:T(1,128)} %bitcast.11, bf16[3,3,128,2048]{3,2,1,0:T(8,128)(2,1)} %w_update.1, bf16[3,3,128,2048]{3,2,1,0:T(8,128)(2,1)} %w_reset.1, ...), custom_call_target="tpu_custom_call" | custom-call | tf_op jit(solution)/shard_map/pallas_call | solution.py:431
  55.4 1.6 %copy.10 = bf16[128,4,128]{2,1,0:T(4,128)(2,1)} copy(bf16[128,4,128]{2,1,0:T(4,128)(2,1)} %bitcast.6) | data formatting | bytes 262144

commit v2 on v1

--- a/solution.py
+++ b/solution.py
@@ -40,7 +40,7 @@
         pltpu.make_async_copy(src, weights.at[i], w_sem.at[i])
         for i, src in enumerate((w_reset, w_update, w_cand))
     ]
-    for copy in raw_copies + w_copies:
+    for copy in raw_copies:
         copy.start()
 
     def ident(l, p):
@@ -80,8 +80,11 @@
         ],
         0,
     ).astype(raw.dtype)
-    for i, copy in enumerate(raw_copies):
+    for copy in raw_copies:
         copy.wait()
+    for copy in w_copies:
+        copy.start()
+    for i in range(2):
         planes = jnp.dot(to_planes, raw[i], preferred_element_type=f32).astype(raw.dtype)
         for r in range(rows):
             joined[i, slot(r), mine] = planes[r * n : (r + 1) * n]
@@ -106,7 +109,7 @@
             return pltpu.make_async_remote_copy(
                 src_ref=ref,
                 dst_ref=ref,
-                send_sem=self.send.at[way, c, part, h],
+                send_sem=self.send.at[way, c],
                 recv_sem=self.band_sem.at[c, part, h],
                 device_id={"chan": (up, down, partner)[way]},
                 device_id_type=MESH,
@@ -116,8 +119,8 @@
             return pltpu.make_async_remote_copy(
                 src_ref=self.buf.at[h, side, block(c)],
                 dst_ref=self.buf.at[h, rows + 1 - side, block(c)],
-                send_sem=self.send.at[3 + side, c, EDGE, h],
-                recv_sem=self.rim_sem.at[side, c, h],
+                send_sem=self.send.at[3 + side, c],
+                recv_sem=self.rim_sem.at[side, c],
                 device_id={"rows": row - 1 if side == 0 else row + 1},
                 device_id_type=MESH,
             )
@@ -175,34 +178,54 @@
                             self.band(2, c, EDGE, h).wait_recv()
                         self.rims(c, h, act)
 
+        def all_of(self, sem, slots, c):
+            ref = self.buf.at[:, slots, block(c)]
+            return pltpu.make_async_copy(ref, ref, sem)
+
         def rims_in(self, c):
-            for h in self.kinds:
-                @pl.when(has_below)
+            for side, there in ((0, has_below), (1, has_above)):
+                @pl.when(there)
                 def _():
-                    self.rim(0, c, h).wait_recv()
-
-                @pl.when(has_above)
-                def _():
-                    self.rim(1, c, h).wait_recv()
+                    slots = pl.ds(rows + 1 - side, 1)
+                    self.all_of(self.rim_sem.at[side, c], slots, c).wait()
 
         def inner_in(self, c):
             for h in self.kinds:
                 self.band(2, c, INNER, h).wait_recv()
 
+        def sent(self, way, slots, c):
+            self.all_of(self.send.at[way, c], slots, c).wait()
+
         def finish(self):
-            for part in (EDGE, INNER):
-                self.begin(done, part)
+            ways = ((has_up, 0), (has_down, 1))
+            whole, edge, inner = pl.ds(0, rows), pl.ds(0, 2), pl.ds(2, rows - 2)
+            for there, way in ways:
+                @pl.when(there)
+                def _():
+                    self.sent(way, whole, me)
+                    self.sent(way, inner, partner)
+            self.sent(2, whole, me)
             for s in range(1, lines):
-                self.pass_on(s, done, False)
-            self.diagonal(done)
-            for s in range(lines):
-                self.across(s, done, False)
+                for l, (there, way) in zip((line - s, line + s), ways):
+                    c = ident(l, pair)
+
+                    @pl.when((l >= 0) & (l < lines))
+                    def _():
+                        self.sent(2, edge if s == 1 else whole, c)
+
+                    @pl.when((l >= 0) & (l < lines) & there)
+                    def _():
+                        self.sent(way, whole, c)
+
+            @pl.loop(0, n_chan)
+            def _(c):
+                for there, side in ((has_above, 0), (has_below, 1)):
+                    @pl.when(there)
+                    def _():
+                        self.sent(3 + side, pl.ds(side, 1), c)
 
     def start(copy):
         copy.start()
-
-    def done(copy):
-        copy.wait_send()
 
     def sides(s, body):
         @pl.loop(0, 2)
@@ -444,12 +467,12 @@
             pltpu.VMEM((3, n, cols), f32),
             dma((2,)),
             dma((3,)),
-            dma((5, n_chan, 2, 2)),
+            dma((5, n_chan)),
             dma((n_chan, 2, 2)),
-            dma((2, n_chan, 2)),
-            dma((5, n_chan, 2, 1)),
+            dma((2, n_chan)),
+            dma((5, n_chan)),
             dma((n_chan, 2, 1)),
-            dma((2, n_chan, 1)),
+            dma((2, n_chan)),
         ],
         compiler_params=pltpu.CompilerParams(
             collective_id=0, has_side_effects=True, vmem_limit_bytes=60 * 1024 * 1024

time: 57.2 us -> 53 us (0.927)
  Pallas kernels: 55.4 us -> 51.3 us
    pallas_call x1, Pallas kernels: 55.4 us -> 51.3 us  [per_device(): pl.pallas_call(functools.partial(kernel, n_chan, n_rows, rows), out_shape...]
where the time goes in v2:
time: 53 us; the launch traced here: 52.9 us
  Pallas kernels  51.3 us (97%)
  local copies, waits for them, and re-layouts  1.61 us (3%)
    pallas_call x1, Pallas kernels, per_device(): pl.pallas_call(functools.partial(kernel, n_chan, n_rows, rows), out_shape...  51.3 us
    unnamed x1, local copies, waits for them, and re-layouts  1.61 us

profile of v2, /device:TPU:1, one launch (start us, length us, event | category | flops | bytes accessed | tf_op | source)
XLA Modules:
  0.0 52.9 jit_solution(17057606767361494054)
XLA Ops:
  0.0 51.3 %shard_map.82 = bf16[512,128]{1,0:T(8,128)(2,1)} custom-call(bf16[512,128]{1,0:T(8,128)(2,1)} %bitcast.7, bf16[512,128]{1,0:T(8,128)(2,1)} %bitcast.8, f32[1,128]{1,0:T(1,128)} %bitcast.9, f32[1,128]{1,0:T(1,128)} %bitcast.10, f32[1,128]{1,0:T(1,128)} %bitcast.11, bf16[3,3,128,2048]{3,2,1,0:T(8,128)(2,1)} %w_update.1, bf16[3,3,128,2048]{3,2,1,0:T(8,128)(2,1)} %w_reset.1, ...), custom_call_target="tpu_custom_call" | custom-call | tf_op jit(solution)/shard_map/pallas_call | solution.py:454
  51.3 1.6 %copy.10 = bf16[128,4,128]{2,1,0:T(4,128)(2,1)} copy(bf16[128,4,128]{2,1,0:T(4,128)(2,1)} %bitcast.6) | data formatting | bytes 262144

commit v3 on v2

--- a/solution.py
+++ b/solution.py
@@ -28,6 +28,7 @@
     row = lax.axis_index("rows")
     line, pair = me // PAIR, me % PAIR
     has_up, has_down = line < lines - 1, line > 0
+    at_end = (line == 0) | (line == lines - 1)
     has_above, has_below = row > 0, row < n_rows - 1
     eager = n % WIDE == 0
     f32 = jnp.float32
@@ -47,6 +48,8 @@
         return l * PAIR + p
 
     up, down, partner = ident(line + 1, pair), ident(line - 1, pair), ident(line, 1 - pair)
+    far_end = ident(lines - 1 - line, pair)
+    to_far = at_end if lines > 2 else line < 0
     barrier = pltpu.get_barrier_semaphore()
 
     def greet(there, target):
@@ -57,6 +60,7 @@
     pl.semaphore_signal(barrier, inc=1, device_id={"chan": partner}, device_id_type=MESH)
     greet(has_up, {"chan": up})
     greet(has_down, {"chan": down})
+    greet(to_far, {"chan": far_end})
     greet(has_above, {"rows": row - 1})
     greet(has_below, {"rows": row + 1})
 
@@ -94,6 +98,7 @@
         1
         + has_up.astype(jnp.int32)
         + has_down.astype(jnp.int32)
+        + to_far.astype(jnp.int32)
         + has_above.astype(jnp.int32)
         + has_below.astype(jnp.int32),
     )
@@ -101,24 +106,30 @@
     class Mover:
         def __init__(self, buf, send, band_sem, rim_sem):
             self.buf, self.send, self.band_sem, self.rim_sem = buf, send, band_sem, rim_sem
-            self.kinds = range(buf.shape[0])
-
-        def band(self, way, c, part, h):
+            self.kinds = range(2)
+
+        def half(self, slots, c, h):
+            if self.buf.shape[0] == 2:
+                return self.buf.at[h, slots, block(c)]
+            few = n // 2
+            return self.buf.at[0, slots, pl.ds(pl.multiple_of(c * n + h * few, few), few)]
+
+        def band(self, way, c, part, h, target=None):
             slots = pl.ds(0, 2) if part == EDGE else pl.ds(2, rows - 2)
-            ref = self.buf.at[h, slots, block(c)]
+            ref = self.half(slots, c, h)
             return pltpu.make_async_remote_copy(
                 src_ref=ref,
                 dst_ref=ref,
                 send_sem=self.send.at[way, c],
                 recv_sem=self.band_sem.at[c, part, h],
-                device_id={"chan": (up, down, partner)[way]},
+                device_id={"chan": (up, down, partner)[way] if target is None else target},
                 device_id_type=MESH,
             )
 
         def rim(self, side, c, h):
             return pltpu.make_async_remote_copy(
-                src_ref=self.buf.at[h, side, block(c)],
-                dst_ref=self.buf.at[h, rows + 1 - side, block(c)],
+                src_ref=self.half(pl.ds(side, 1), c, h),
+                dst_ref=self.half(pl.ds(rows + 1 - side, 1), c, h),
                 send_sem=self.send.at[3 + side, c],
                 recv_sem=self.rim_sem.at[side, c],
                 device_id={"rows": row - 1 if side == 0 else row + 1},
@@ -148,34 +159,45 @@
                 for h in self.kinds:
                     self.rims(me, h, act)
 
-        def pass_on(self, s, act, first):
-            for part in (EDGE, INNER):
-                for h in self.kinds:
-                    for way, l in ((0, line - s), (1, line + s)):
-                        @pl.when((l >= 0) & (l < lines))
+        def pass_on(self, s, part, act):
+            for h in self.kinds:
+                for way, l, end in ((0, line - s, 0), (1, line + s, lines - 1)):
+                    c = ident(l, pair)
+                    there = (l >= 0) & (l < lines)
+
+                    @pl.when(there)
+                    def _():
+                        self.band(2, c, part, h).wait_recv()
+                        self.along(way, c, part, h, act)
+                        if part == INNER or s not in (1, lines - 1):
+                            act(self.band(2, c, part, h))
+
+                    if part == EDGE and s == 1 and lines > 2:
+                        @pl.when(there & (l != end))
                         def _():
-                            c = ident(l, pair)
-                            if first:
-                                self.band(2, c, part, h).wait_recv()
-                            self.along(way, c, part, h, act)
-                            if part == EDGE or s > 1:
-                                act(self.band(2, c, part, h))
-                            if part == EDGE:
-                                self.rims(c, h, act)
+                            act(self.band(2, c, part, h))
+
+                    if part == EDGE:
+                        @pl.when(there)
+                        def _():
+                            self.rims(c, h, act)
 
         def diagonal(self, act):
             for h in self.kinds:
-                self.along(0, partner, INNER, h, act)
-                self.along(1, partner, INNER, h, act)
-
-        def across(self, s, act, first):
+                for way, end in ((0, 0), (1, lines - 1)):
+                    @pl.when(line == end)
+                    def _():
+                        act(self.band(way, partner, EDGE, h))
+                        if lines > 2:
+                            act(self.band(1 - way, partner, EDGE, h, far_end))
+
+        def across(self, s, act):
             for l in (line - s, line + s)[: 1 if s == 0 else 2]:
                 @pl.when((l >= 0) & (l < lines))
                 def _():
                     c = ident(l, 1 - pair)
                     for h in self.kinds:
-                        if first:
-                            self.band(2, c, EDGE, h).wait_recv()
+                        self.band(2, c, EDGE, h).wait_recv()
                         self.rims(c, h, act)
 
         def all_of(self, sem, slots, c):
@@ -203,15 +225,23 @@
                 @pl.when(there)
                 def _():
                     self.sent(way, whole, me)
-                    self.sent(way, inner, partner)
+
+                @pl.when(at_end if lines > 2 else at_end & there)
+                def _():
+                    self.sent(way, edge, partner)
             self.sent(2, whole, me)
             for s in range(1, lines):
-                for l, (there, way) in zip((line - s, line + s), ways):
+                for l, end, (there, way) in zip((line - s, line + s), (0, lines - 1), ways):
                     c = ident(l, pair)
-
-                    @pl.when((l >= 0) & (l < lines))
+                    short = l == end if s in (1, lines - 1) else l < 0
+
+                    @pl.when((l >= 0) & (l < lines) & short)
                     def _():
-                        self.sent(2, edge if s == 1 else whole, c)
+                        self.sent(2, inner, c)
+
+                    @pl.when((l >= 0) & (l < lines) & jnp.logical_not(short))
+                    def _():
+                        self.sent(2, whole, c)
 
                     @pl.when((l >= 0) & (l < lines) & there)
                     def _():
@@ -291,13 +321,11 @@
     def new_on(at, width):
         acc_cand[...] += product(2, 1, ((channels, rh, 0),), at, width)
 
-    last = sorted({1, lines - 1})
-
-    def near(s):
+    def near(s, compute):
         def body(l):
             c = ident(l, pair)
             first.rims_in(c)
-            gates_on(c)
+            compute(c)
 
         sides(s, body)
 
@@ -311,15 +339,15 @@
         sides(s, body)
 
     for s in range(1, lines):
-        first.pass_on(s, start, True)
-        if s == max(1, lines - 2):
-            if s == 1:
-                first.inner_in(partner)
+        first.pass_on(s, EDGE, start)
+        first.across(s - 1, start)
+        if s == 1:
             first.diagonal(start)
-        first.across(s - 1, start, True)
+        if s == lines - 1:
+            first.across(s, start)
+        first.pass_on(s, INNER, start)
         if s == 1:
-            if lines > 3:
-                first.inner_in(partner)
+            first.inner_in(partner)
             w_copies[0].wait()
             w_copies[1].wait()
             if eager:
@@ -328,14 +356,11 @@
                 first.rims_in(partner)
                 gates_on(partner)
         elif eager:
-            near(s - 1)
-            if s > 2:
-                far(s - 1, gates_on)
-    first.across(lines - 1, start, True)
+            near(s - 1, gates_on)
+            far(s - 1, gates_on)
     if eager:
-        near(lines - 1)
-        for s in last:
-            far(s, reset_on)
+        near(lines - 1, reset_on)
+        far(lines - 1, reset_on)
     else:
         for s in range(1, lines):
             sides(s, lambda l: first.inner_in(ident(l, 1 - pair)))
@@ -367,19 +392,18 @@
         second.begin(start, part)
 
     if eager:
-        for s in last:
-            sides(s, lambda l: update_on(ident(l, 1 - pair)))
+        @pl.loop(0, PAIR)
+        def _(p):
+            sides(lines - 1, lambda l: update_on(ident(l, p)))
     w_copies[2].wait()
-
-    def older():
-        width = PAIR * n if eager else WIDE
-
-        @pl.loop(0, channels // width)
-        def _(g):
-            old_on(g * width, width)
-
-        for r in range(rows):
-            gate[r] = jax.nn.sigmoid(folded(acc, 1, r) + bias[1])
+    width = PAIR * n if eager else WIDE
+
+    @pl.loop(0, channels // width)
+    def _(g):
+        old_on(g * width, width)
+
+    for r in range(rows):
+        gate[r] = jax.nn.sigmoid(folded(acc, 1, r) + bias[1])
 
     def both_on(l):
         for p in range(PAIR):
@@ -394,24 +418,23 @@
         sides(s, body)
 
     for s in range(1, lines):
-        second.pass_on(s, start, True)
-        if s == max(1, lines - 2):
-            if s == 1:
-                second.inner_in(partner)
+        second.pass_on(s, EDGE, start)
+        second.across(s - 1, start)
+        if s == 1:
             second.diagonal(start)
-        second.across(s - 1, start, True)
+        if s == lines - 1:
+            second.across(s, start)
+        second.pass_on(s, INNER, start)
         if s == 1:
-            if lines > 3:
-                second.inner_in(partner)
-            older()
-            if eager:
-                both_on(line)
-        elif eager and s > 2:
+            second.inner_in(partner)
+        if not eager:
+            continue
+        if s == 1:
+            both_on(line)
+        else:
             both_far(s - 1)
-    second.across(lines - 1, start, True)
     if eager:
-        for s in last:
-            both_far(s)
+        both_far(lines - 1)
     else:
         for s in range(1, lines):
             sides(s, lambda l: second.inner_in(ident(l, 1 - pair)))
@@ -471,7 +494,7 @@
             dma((n_chan, 2, 2)),
             dma((2, n_chan)),
             dma((5, n_chan)),
-            dma((n_chan, 2, 1)),
+            dma((n_chan, 2, 2)),
             dma((2, n_chan)),
         ],
         compiler_params=pltpu.CompilerParams(

time: 53 us -> 50.9 us (0.960)
  the two profiles are of different devices: /device:TPU:1 before, /device:TPU:0 now
where the time goes in v3:
time: 50.9 us; the launch traced here: 50.8 us
  Pallas kernels  49.2 us (97%)
  local copies, waits for them, and re-layouts  1.61 us (3%)
    pallas_call x1, Pallas kernels, per_device(): pl.pallas_call(functools.partial(kernel, n_chan, n_rows, rows), out_shape...  49.2 us
    unnamed x1, local copies, waits for them, and re-layouts  1.61 us

profile of v3, /device:TPU:0, one launch (start us, length us, event | category | flops | bytes accessed | tf_op | source)
XLA Modules:
  0.0 50.8 jit_solution(1644333421104066317)
XLA Ops:
  0.0 49.2 %shard_map.82 = bf16[512,128]{1,0:T(8,128)(2,1)} custom-call(bf16[512,128]{1,0:T(8,128)(2,1)} %bitcast.7, bf16[512,128]{1,0:T(8,128)(2,1)} %bitcast.8, f32[1,128]{1,0:T(1,128)} %bitcast.9, f32[1,128]{1,0:T(1,128)} %bitcast.10, f32[1,128]{1,0:T(1,128)} %bitcast.11, bf16[3,3,128,2048]{3,2,1,0:T(8,128)(2,1)} %w_update.1, bf16[3,3,128,2048]{3,2,1,0:T(8,128)(2,1)} %w_reset.1, ...), custom_call_target="tpu_custom_call" | custom-call | tf_op jit(solution)/shard_map/pallas_call | solution.py:477
  49.2 1.6 %copy.10 = bf16[128,4,128]{2,1,0:T(4,128)(2,1)} copy(bf16[128,4,128]{2,1,0:T(4,128)(2,1)} %bitcast.6) | data formatting | bytes 262144
